TPU v7x, 32 devices: a whole 2x2x4 slice. The times are simulated.
32 devices in a mesh: blk: 16 (over z, x, core), rep: 2 (over y).
Axes of the slice: x: 2, y: 2, z: 4, core: 2. Of those that a mesh axis runs over, the one named last changes fastest.
Arguments:
- features: bfloat16 [4096, 128], P(('blk', 'rep')), may hold values from -6 to 6
- tile_mask: int32 [32, 32], P('blk'), may hold values 0 or 1
- multiplicity: int32 [32, 32], P('blk'), may hold values from 1 to 4
- w_query: bfloat16 [128, 128], replicated, may hold values from -0.5 to 0.5
- w_value: bfloat16 [128, 128], replicated, may hold values from -0.5 to 0.5
Outputs:
- updated: bfloat16 [4096, 128], P(('blk', 'rep'))
All inputs are finite; a program needn't handle non-finite values. No bound on the sum of `tile_mask` on one device may be relied on, other than what follows from the above.
Results may differ from a plain program's by a relative error of at most 0.0057.
Values may be sent and summed in bfloat16 or wider, within the bound.
A program may use at most 64 MiB of HBM per device.

v0:
```python
import math

import jax
import jax.numpy as jnp
from jax import lax
from jax.sharding import PartitionSpec as P

TILE = 128


def body(features, tile_mask, multiplicity, w_query, w_value):
    src_rows = features.shape[0]
    cycle_count = lax.axis_size("blk")
    rep_count = lax.axis_size("rep")
    rep_index = lax.axis_index("rep")
    own_query = jnp.dot(features, w_query, preferred_element_type=jnp.float32).astype(jnp.bfloat16)
    queries = lax.all_gather(own_query, "rep", axis=0, tiled=True)
    tgt_rows = queries.shape[0]
    tgt_tiles = tgt_rows // TILE
    src_tiles = src_rows // TILE
    factor = (tile_mask * multiplicity).astype(jnp.float32)
    factor = factor.reshape(tgt_tiles, cycle_count, rep_count, src_tiles)
    factor = lax.dynamic_index_in_dim(factor, rep_index, 2, keepdims=False)
    root_scale = 1.0 / features.shape[1] ** 0.5

    def absorb_tiles(partial_value, source, tile_factor):
        count_rows = source.shape[0]
        scores = (
            lax.dot_general(
                queries, source, (((1,), (1,)), ((), ())), preferred_element_type=jnp.float32
            )
            * root_scale
        )
        scores = jnp.where(scores > 0, scores, 0.2 * scores)
        weights = (
            scores.reshape(tgt_tiles, TILE, count_rows // TILE, TILE)
            * tile_factor[:, None, :, None]
        )
        weights = weights.reshape(tgt_rows, count_rows).astype(jnp.bfloat16)
        return partial_value + jnp.dot(weights, source, preferred_element_type=jnp.float32)

    start = jnp.zeros((tgt_rows, features.shape[1]), jnp.float32)
    flat_factor = factor.reshape(tgt_tiles, cycle_count * src_tiles)
    piece = lax.all_gather(features, "blk", axis=0, tiled=True)
    piece_rows = piece.shape[0]
    step_rows = math.gcd(piece_rows, max(src_rows, 1024))
    step_count = piece_rows // step_rows
    piece_blocks = piece.reshape(step_count, step_rows, piece.shape[1])

    def one_part(carry, index_pair):
        part_rows, part_index = index_pair
        first_tile = part_index * step_rows // TILE
        tile_factor = lax.dynamic_slice_in_dim(flat_factor, first_tile, step_rows // TILE, 1)
        return (absorb_tiles(carry, part_rows, tile_factor), None)

    result, unused = lax.scan(
        one_part, start, (piece_blocks, jnp.arange(step_count, dtype=jnp.int32))
    )
    partial_value = result
    summed = lax.psum_scatter(partial_value, "rep", scatter_dimension=0, tiled=True)
    total_verts = src_rows * cycle_count * rep_count
    aggregate = (summed * (2.0 * total_verts) ** (-0.5)).astype(jnp.bfloat16)
    mixed = jnp.dot(aggregate, w_value, preferred_element_type=jnp.float32)
    return (features.astype(jnp.float32) + mixed).astype(jnp.bfloat16)


def solution(mesh):
    in_specs = (P(("blk", "rep"), None), P("blk", None), P("blk", None), P(), P())
    out_specs = P(("blk", "rep"), None)
    return jax.shard_map(body, mesh=mesh, in_specs=in_specs, out_specs=out_specs, check_vma=False)
```

profile of v0, /device:TPU:0, one launch (start us, length us, event | category | flops | bytes accessed | tf_op | source)
XLA Modules:
  0.0 58.8 jit_solution(14389451639451653202)
XLA Ops:
  6.5 0.0 copy-start
  6.5 0.0 reduce-scatter.2.cloned.1.call-start
  6.6 0.7 %copy-done.5 = s32[2,32]{1,0:T(2,128)S(1)} copy-done((s32[2,32]{1,0:T(2,128)S(1)}, s32[2,32]{1,0:T(2,128)}, u32[]{:S(2)}) %copy-start.5) | copy-done | bytes 280
  7.2 0.0 copy-done.4
  7.3 0.1 reshape.20
  7.3 0.1 constant_dynamic-slice_fusion.1
  7.4 0.2 copy.8
  7.6 0.5 copy-done.1
  8.1 24.6 %all_gather.6 = bf16[2048,128]{1,0:T(8,128)(2,1)S(1)} all-gather(bf16[128,128]{1,0:T(8,128)(2,1)S(1)} %copy-done.1), channel_id=1, replica_groups=mesh['blk'=16,'rep'=2] {'blk'}, dimensions={0}, use_global_device_ids=true | all-gather | bytes 557056 | tf_op jit(solution)/shard_map/all_gather | solution.py:44
  32.7 0.0 copy-done
  32.7 0.1 convolution_convert_fusion
  32.8 4.6 %all_gather.7 = bf16[256,128]{1,0:T(8,128)(2,1)S(1)} all-gather(bf16[128,128]{1,0:T(8,128)(2,1)S(1)} %convolution_convert_fusion), channel_id=1, replica_groups=mesh['blk'=16,'rep'=2] {'rep'}, dimensions={0}, use_global_device_ids=true | all-gather | bytes 98304 | tf_op jit(solution)/shard_map/all_gather | solution.py:17
  37.4 4.4 %while.13 = (s32[]{:T(128)}, f32[256,128]{1,0:T(8,128)S(1)}, bf16[2,1024,128]{2,1,0:T(8,128)(2,1)S(1)}, bf16[256,128]{1,0:T(8,128)(2,1)S(1)}, s32[2]{0:T(128)S(1...) while((s32[]{:T(128)}, f32[256,128]{1,0:T(8,128)S(1)}, ...), condition=%wide.region_1.2_spmd.clone, body=%wide.region_0.1_spmd.clone.sunk | while | flops 135856144 | bytes 2950683 | solution.py:56
  37.4 0.6 dynamic_slice.44
  38.6 0.3 mul.98
  38.9 0.7 %convolution_add_fusion.3 = f32[256,128]{1,0:T(8,128)S(1)} fusion(f32[128,8,2,128]{3,2,1,0:T(2,128)S(1)} %bitcast.43, bf16[256,128]{1,0:T(8,128)(2,1)S(1)} %get-tuple-element.196, bf16[2,1024,128]{2,1,0:T(8,128)(2,1)S(1)} %get-tuple-element.195, s32[]{:T(128)} %get-tuple-element.180, f32[256,128]{1,0:T(8,128)S(1)} %get-tuple-element.181, pred[]{:T(512)S(6)} %compare.9), kind=kOutput, calls=%fused_computation.1.clone.1 | convolution fusion | flops 135856128 | bytes 1901569 | tf_op jit(solution)/shard_map/while/body/eval_jaxpr/dot_general | solution.py:40
  39.6 0.6 dynamic_slice.44
  40.8 0.3 mul.98
  41.2 0.7 %convolution_add_fusion.3 = f32[256,128]{1,0:T(8,128)S(1)} fusion(f32[128,8,2,128]{3,2,1,0:T(2,128)S(1)} %bitcast.43, bf16[256,128]{1,0:T(8,128)(2,1)S(1)} %get-tuple-element.196, bf16[2,1024,128]{2,1,0:T(8,128)(2,1)S(1)} %get-tuple-element.195, s32[]{:T(128)} %get-tuple-element.180, f32[256,128]{1,0:T(8,128)S(1)} %get-tuple-element.181, pred[]{:T(512)S(6)} %compare.9), kind=kOutput, calls=%fused_computation.1.clone.1 | convolution fusion | flops 135856128 | bytes 1901569 | tf_op jit(solution)/shard_map/while/body/eval_jaxpr/dot_general | solution.py:40
  41.9 0.0 copy-start.3
  41.9 0.6 %copy-done.2 = f32[256,128]{1,0:T(8,128)} copy-done((f32[256,128]{1,0:T(8,128)}, f32[256,128]{1,0:T(8,128)S(1)}, u32[]{:S(2)}) %copy-start.2) | copy-done | bytes 131096
  42.5 0.0 reduce-scatter.2.cloned.1.call-update
  42.5 7.8 %reduce-scatter.2.cloned.1.call-done = f32[128,128]{1,0:T(8,128)} async-done(((f32[256,128]{1,0:T(8,128)}), f32[128,128]{1,0:T(8,128)}) %reduce-scatter.2.cloned.1.call-update) | async-done | bytes 65552 | tf_op jit(solution)/shard_map/reduce_scatter | solution.py:60
  50.3 1.6 %fusion.14 = bf16[128,128]{1,0:T(8,128)(2,1)} fusion(bf16[128,128]{1,0:T(8,128)(2,1)S(1)} %copy-done.3, bf16[128,128]{1,0:T(8,128)(2,1)S(1)} %copy-done.1, f32[128,128]{1,0:T(8,128)} %reduce-scatter.2.cloned.1.call-done), kind=kOutput, calls=%fused_computation.15 | convolution fusion | flops 4276224 | bytes 163840 | tf_op jit(solution)/shard_map/dot_general | solution.py:63
  (10 shorter events, 0.0 us)
Async XLA Ops:
  6.5 26.2 %copy-start = (bf16[128,128]{1,0:T(8,128)(2,1)S(1)}, bf16[128,128]{1,0:T(8,128)(2,1)}, u32[]{:S(2)}) copy-start(bf16[128,128]{1,0:T(8,128)(2,1)} %param.10) | copy-start | bytes 98308
  6.5 43.8 %reduce-scatter.2.cloned.1.call-start = ((), (), s32[]{:S(2)}) async-start(), calls=%async_computation.1 | async-start | bytes 196608 | tf_op jit(solution)/shard_map/reduce_scatter | solution.py:60
  6.5 0.7 %copy-start.5 = (s32[2,32]{1,0:T(2,128)S(1)}, s32[2,32]{1,0:T(2,128)}, u32[]{:S(2)}) copy-start(s32[2,32]{1,0:T(2,128)} %param.9) | copy-start | bytes 772
  6.5 0.7 %copy-start.4 = (s32[2,32]{1,0:T(2,128)S(1)}, s32[2,32]{1,0:T(2,128)}, u32[]{:S(2)}) copy-start(s32[2,32]{1,0:T(2,128)} %param.8) | copy-start | bytes 772
  7.3 0.8 %copy-start.1 = (bf16[128,128]{1,0:T(8,128)(2,1)S(1)}, bf16[128,128]{1,0:T(8,128)(2,1)}, u32[]{:S(2)}) copy-start(bf16[128,128]{1,0:T(8,128)(2,1)} %param.7) | copy-start | bytes 98308
  41.8 0.7 %copy-start.2 = (f32[256,128]{1,0:T(8,128)}, f32[256,128]{1,0:T(8,128)S(1)}, u32[]{:S(2)}) copy-start(f32[256,128]{1,0:T(8,128)S(1)} %get-tuple-element.84) | copy-start | bytes 393220
  41.9 8.5 %copy-start.3 = (bf16[128,128]{1,0:T(8,128)(2,1)S(1)}, bf16[128,128]{1,0:T(8,128)(2,1)}, u32[]{:S(2)}) copy-start(bf16[128,128]{1,0:T(8,128)(2,1)} %param.11) | copy-start | bytes 98308
Sparse Core Ops, SparseCore 0:
  42.6 7.6 reduce-scatter.1
where the time goes:
time: 59.1 us; the launch traced here: 58.8 us
  blocking collectives  29.2 us (49%)
  between operations  13.4 us (23%)
  waiting for transfers between devices  7.82 us (13%)
  local copies, waits for them, and re-layouts  4.05 us (7%)
  matrix products  3.05 us (5%)
  loops' own time  1.24 us (2%)
    all_gather x1, blocking collectives, body(): piece = lax.all_gather(features, 'blk', axis=0, tiled=True)  24.6 us
    reduce_scatter x1, waiting for transfers between devices, body(): lax.psum_scatter(partial_value, 'rep', scatter_dimension=0, tiled=True)  7.8 us
    all_gather x1, blocking collectives, body(): queries = lax.all_gather(own_query, 'rep', axis=0, tiled=True)  4.58 us
    unnamed x13, local copies, waits for them, and re-layouts  2.02 us
    dot_general x1, matrix products, body(): mixed = jnp.dot(aggregate, w_value, preferred_element_type=jnp.float32)  1.59 us
    dot_general x2, matrix products, absorb_tiles(): jnp.dot(weights, source, preferred_element_type=jnp.float32)  1.33 us
    another operation x1, loops' own time, body(): lax.scan(one_part, start, (piece_blocks, jnp.arange(step_count, dtype=jnp...  1.24 us
  transfers between devices with their start and end apart: 1, of which 1 were waited for; matrix products, arithmetic and copies ran while one was open for 0% of the time, Pallas kernels for 0%

commit v1 on v0

v1 whole, which is shorter than its diff:
```python
import functools
import itertools

import jax
import jax.numpy as jnp
from jax import lax
from jax.experimental import pallas as pl
from jax.experimental.pallas import tpu as pltpu
from jax.sharding import PartitionSpec as P

TILE = 128
MESH = pl.DeviceIdType.MESH


def split_of(blk_count):
    cores = 2 if blk_count % 2 == 0 else 1
    mids = 2 if (blk_count // cores) % 2 == 0 else 1
    return blk_count // (cores * mids), mids, cores


def kernel(
    blk_count, rep_count,
    x_hbm, mask_hbm, mult_hbm, wq_hbm, wv_hbm,
    out_ref,
    tgt, src, masks, mults, wq, wv, factors, weights_acc, sums, sent, got,
    local_sems, tgt_send, tgt_recv, src_send, src_recv, tab_send, tab_recv, sum_send, sum_recv,
):
    fars, mids, cores = split_of(blk_count)
    b = lax.axis_index("blk")
    r = lax.axis_index("rep")
    core = b % cores
    mid = (b // cores) % mids
    far = b // (cores * mids)
    near = list(itertools.product(range(mids), range(cores), range(rep_count)))
    tables = list(itertools.product(range(mids), range(cores)))
    near_count = len(near)

    def near_id(dm, dc, dr):
        m, c, q = (mid + dm) % mids, (core + dc) % cores, (r + dr) % rep_count
        return ((far * mids + m) * cores + c, q)

    def far_id(dh):
        return ((((far + dh) % fars) * mids + mid) * cores + core, r)

    def near_slot(dm, dc, dr):
        return near.index((-dm % mids, -dc % cores, -dr % rep_count))

    barrier = pltpu.get_barrier_semaphore()
    for dh in range(1, fars):
        pl.semaphore_signal(barrier, inc=1, device_id=far_id(dh), device_id_type=MESH)
    for offset in near[1:]:
        pl.semaphore_signal(barrier, inc=1, device_id=near_id(*offset), device_id_type=MESH)
    local = [
        pltpu.make_async_copy(x_hbm, src.at[0], local_sems.at[0]),
        pltpu.make_async_copy(wq_hbm, wq, local_sems.at[1]),
        pltpu.make_async_copy(wv_hbm, wv, local_sems.at[2]),
        pltpu.make_async_copy(mask_hbm, masks.at[0], local_sems.at[3]),
        pltpu.make_async_copy(mult_hbm, mults.at[0], local_sems.at[4]),
    ]
    for copy in local:
        copy.start()
    pl.semaphore_wait(barrier, fars - 1 + near_count - 1)

    copies = []
    for dh in sorted(range(1, fars), key=lambda d: -min(d, fars - d)):
        copies.append(pltpu.make_async_remote_copy(
            src_ref=x_hbm, dst_ref=src.at[-dh % fars],
            send_sem=src_send.at[dh], recv_sem=src_recv.at[-dh % fars],
            device_id=far_id(dh), device_id_type=MESH))
    for k, (dm, dc) in enumerate(tables):
        if k:
            slot = tables.index((-dm % mids, -dc % cores))
            for n, (table, slots) in enumerate(((mask_hbm, masks), (mult_hbm, mults))):
                copies.append(pltpu.make_async_remote_copy(
                    src_ref=table, dst_ref=slots.at[slot],
                    send_sem=tab_send.at[n, k], recv_sem=tab_recv.at[n, slot],
                    device_id=near_id(dm, dc, 0), device_id_type=MESH))
    for k, offset in enumerate(near):
        if k:
            slot = near_slot(*offset)
            copies.append(pltpu.make_async_remote_copy(
                src_ref=x_hbm, dst_ref=tgt.at[slot],
                send_sem=tgt_send.at[k], recv_sem=tgt_recv.at[slot],
                device_id=near_id(*offset), device_id_type=MESH))
    for copy in copies:
        copy.start()

    def arrived(dst, sem):
        pltpu.make_async_copy(dst, dst, sem).wait()

    for copy in local:
        copy.wait()
    root_scale = 1.0 / x_hbm.shape[1] ** 0.5
    width = fars * TILE
    tile_count = masks.shape[2]

    def expand():
        place = lax.broadcasted_iota(jnp.int32, (tile_count, width), 1) // TILE
        f = far + place
        f = jnp.where(f >= fars, f - fars, f)
        tile = ((f * mids + mid) * cores + core) * rep_count + r
        one_hot = (lax.broadcasted_iota(jnp.int32, (tile_count, width), 0) == tile)
        return one_hot.astype(jnp.float32).astype(jnp.bfloat16)

    def query_of(rows):
        return jnp.dot(rows, wq[...], preferred_element_type=jnp.float32).astype(jnp.bfloat16)

    def weigh(query, source, factor):
        score = lax.dot_general(query, source, (((1,), (1,)), ((), ())),
                                preferred_element_type=jnp.float32)
        score = score * factor
        return jnp.maximum(score, 0.2 * score).astype(jnp.bfloat16)

    one_hot = expand()
    for k, (dm, dc) in enumerate(tables):
        if k:
            arrived(masks.at[k], tab_recv.at[0, k])
            arrived(mults.at[k], tab_recv.at[1, k])
        fac = (masks[k] * mults[k]).astype(jnp.float32).astype(jnp.bfloat16)
        wide = jnp.dot(fac, one_hot, preferred_element_type=jnp.float32) * root_scale
        rows = lax.broadcasted_iota(jnp.int32, wide.shape, 0)
        for dr in range(rep_count):
            row = jnp.sum(jnp.where(rows == (r + dr) % rep_count, wide, 0.0), axis=0, keepdims=True)
            factors[near.index((dm, dc, dr))] = row

    own = src[0]
    for k in range(near_count):
        if k:
            arrived(tgt.at[k], tgt_recv.at[k])
            rows = tgt[k]
        else:
            rows = own
        query = query_of(rows)
        weights_acc[k] = query
        sums[k] = jnp.dot(weigh(query, own, factors[k, :, :TILE]), own,
                          preferred_element_type=jnp.float32)

    for dh in range(1, fars):
        arrived(src.at[dh], src_recv.at[dh])
    others = src[1:].reshape(width - TILE, src.shape[2])
    order = sorted(range(near_count), key=lambda k: (k == 0, -sum(v > 0 for v in near[k])))
    for k in order:
        w = weigh(weights_acc[k], others, factors[k, :, TILE:])
        part = sums[k] + jnp.dot(w, others, preferred_element_type=jnp.float32)
        if k:
            sent[k] = part.astype(jnp.bfloat16)
            slot = near_slot(*near[k])
            copy = pltpu.make_async_remote_copy(
                src_ref=sent.at[k], dst_ref=got.at[slot],
                send_sem=sum_send.at[k], recv_sem=sum_recv.at[slot],
                device_id=near_id(*near[k]), device_id_type=MESH)
            copy.start()
            copies.append(copy)
        else:
            total = part
    for k in range(1, near_count):
        arrived(got.at[k], sum_recv.at[k])
        total = total + got[k].astype(jnp.float32)
    verts = TILE * blk_count * rep_count
    aggregate = (total * (2.0 * verts) ** (-0.5)).astype(jnp.bfloat16)
    mixed = jnp.dot(aggregate, wv[...], preferred_element_type=jnp.float32)
    out_ref[...] = (own.astype(jnp.float32) + mixed).astype(jnp.bfloat16)
    for copy in copies:
        copy.wait_send()


def body(blk_count, rep_count, features, tile_mask, multiplicity, w_query, w_value):
    rows, width = features.shape
    assert rows == TILE
    fars, mids, cores = split_of(blk_count)
    near_count = mids * cores * rep_count
    table_rows, table_cols = tile_mask.shape
    dma = pltpu.SemaphoreType.DMA
    return pl.pallas_call(
        functools.partial(kernel, blk_count, rep_count),
        out_shape=jax.ShapeDtypeStruct((rows, width), jnp.bfloat16),
        in_specs=[pl.BlockSpec(memory_space=pl.ANY)] * 5,
        out_specs=pl.BlockSpec(memory_space=pltpu.VMEM),
        scratch_shapes=[
            pltpu.VMEM((near_count, rows, width), jnp.bfloat16),
            pltpu.VMEM((fars, rows, width), jnp.bfloat16),
            pltpu.VMEM((mids * cores, table_rows, table_cols), jnp.int32),
            pltpu.VMEM((mids * cores, table_rows, table_cols), jnp.int32),
            pltpu.VMEM(w_query.shape, jnp.bfloat16),
            pltpu.VMEM(w_value.shape, jnp.bfloat16),
            pltpu.VMEM((near_count, 1, fars * TILE), jnp.float32),
            pltpu.VMEM((near_count, rows, width), jnp.bfloat16),
            pltpu.VMEM((near_count, rows, width), jnp.float32),
            pltpu.VMEM((near_count, rows, width), jnp.bfloat16),
            pltpu.VMEM((near_count, rows, width), jnp.bfloat16),
            dma((5,)),
            dma((near_count,)), dma((near_count,)),
            dma((fars,)), dma((fars,)),
            dma((2, mids * cores)), dma((2, mids * cores)),
            dma((near_count,)), dma((near_count,)),
        ],
        compiler_params=pltpu.CompilerParams(collective_id=0, has_side_effects=True),
    )(features, tile_mask, multiplicity, w_query, w_value)


def solution(mesh):
    in_specs = (P(("blk", "rep"), None), P("blk", None), P("blk", None), P(), P())
    out_specs = P(("blk", "rep"), None)
    run = functools.partial(body, mesh.shape["blk"], mesh.shape["rep"])
    return jax.shard_map(run, mesh=mesh, in_specs=in_specs, out_specs=out_specs, check_vma=False)
```

time: 59.1 us -> 19.7 us (0.33)
  blocking collectives: 29.2 us -> 0 us
  Pallas kernels: 0 us -> 18.1 us
  between operations: 13.4 us -> 0.01 us
  waiting for transfers between devices: 7.82 us -> 0 us
  matrix products: 3.05 us -> 0 us
  local copies, waits for them, and re-layouts: 4.05 us -> 1.38 us
  loops' own time: 1.24 us -> 0 us
    all_gather x2 -> x0, blocking collectives: 29.2 us -> none  [the longest x1 24.6 us: body(): piece = lax.all_gather(features, 'blk', axis=0, tiled=True)]
    pallas_call x0 -> x1, Pallas kernels: none -> 18.1 us  [body(): pl.pallas_call(functools.partial(kernel, blk_count, rep_count), out_shape...]
    reduce_scatter x1 -> x0, waiting for transfers between devices: 7.8 us -> none  [body(): lax.psum_scatter(partial_value, 'rep', scatter_dimension=0, tiled=True)]
    dot_general x4 -> x0, matrix products: 3.05 us -> none  [the longest x1 1.59 us: body(): mixed = jnp.dot(aggregate, w_value, preferred_element_type=jnp.float32)]
    dynamic_slice x5 -> x0, local copies, waits for them, and re-layouts: 1.26 us -> none  [the longest x2 1.16 us: body(): lax.scan(one_part, start, (piece_blocks, jnp.arange(step_count, dtype=jnp...]
    another operation x1 -> x0, loops' own time: 1.24 us -> none  [body(): lax.scan(one_part, start, (piece_blocks, jnp.arange(step_count, dtype=jnp...]
    mul x2 -> x0, local copies, waits for them, and re-layouts: 0.68 us -> none  [absorb_tiles(): scores.reshape(tgt_tiles, TILE, count_rows // TILE, TILE)]
    unnamed x13 -> x1, local copies, waits for them, and re-layouts: 2.02 us -> 1.38 us
  transfers between devices with their start and end apart: 1 -> 0, of which waited for: 1 -> 0; matrix products, arithmetic and copies ran while one was open for 0% -> 0% of each run, Pallas kernels for 0% -> 0%
where the time goes in v1:
time: 19.7 us; the launch traced here: 19.5 us
  Pallas kernels  18.1 us (92%)
  local copies, waits for them, and re-layouts  1.38 us (7%)
    pallas_call x1, Pallas kernels, body(): pl.pallas_call(functools.partial(kernel, blk_count, rep_count), out_shape...  18.1 us
    unnamed x1, local copies, waits for them, and re-layouts  1.38 us

profile of v1, /device:TPU:0, one launch (start us, length us, event | category | flops | bytes accessed | tf_op | source)
XLA Modules:
  0.0 19.5 jit_solution(12576337984361228487)
XLA Ops:
  0.0 18.1 %shard_map.55 = bf16[128,128]{1,0:T(8,128)(2,1)} custom-call(bf16[128,128]{1,0:T(8,128)(2,1)} %x_hbm.1, s32[2,32]{1,0:T(2,128)} %mask_hbm.1, s32[2,32]{1,0:T(2,128)} %mult_hbm.1, bf16[128,128]{1,0:T(8,128)(2,1)} %wq_hbm.1, bf16[128,128]{1,0:T(8,128)(2,1)} %wv_hbm.1), custom_call_target="tpu_custom_call" | custom-call | tf_op jit(solution)/shard_map/pallas_call | solution.py:174
  18.1 1.4 %copy.7 = bf16[128,128]{1,0:T(8,128)(2,1)} copy(bf16[128,128]{1,0:T(8,128)(2,1)} %shard_map.55) | data formatting | bytes 65536

commit v2 on v1

v2 whole, which is shorter than its diff:
```python
import functools
import itertools

import jax
import jax.numpy as jnp
from jax import lax
from jax.experimental import pallas as pl
from jax.experimental.pallas import tpu as pltpu
from jax.sharding import PartitionSpec as P

TILE = 128
MESH = pl.DeviceIdType.MESH


def split_of(blk_count):
    cores = 2 if blk_count % 2 == 0 else 1
    mids = 2 if (blk_count // cores) % 2 == 0 else 1
    return blk_count // (cores * mids), mids, cores


def kernel(
    blk_count, rep_count,
    x_hbm, mask_hbm, mult_hbm, wq_hbm, wv_hbm,
    out_ref,
    tgt, src, masks, mults, wq, wv, factors, queries, sums, sent, got,
    local_sems, tgt_send, tgt_recv, src_send, src_recv, tab_send, tab_recv, sum_send, sum_recv,
):
    fars, mids, cores = split_of(blk_count)
    b = lax.axis_index("blk")
    r = lax.axis_index("rep")
    core = b % cores
    mid = (b // cores) % mids
    far = b // (cores * mids)
    near = list(itertools.product(range(mids), range(cores), range(rep_count)))
    tables = list(itertools.product(range(mids), range(cores)))
    near_count = len(near)
    top = fars - 1

    def near_id(dm, dc, dr):
        m, c, q = (mid + dm) % mids, (core + dc) % cores, (r + dr) % rep_count
        return ((far * mids + m) * cores + c, q)

    def far_id(h):
        return ((h * mids + mid) * cores + core, r)

    def near_slot(dm, dc, dr):
        return near.index((-dm % mids, -dc % cores, -dr % rep_count))

    local = [
        pltpu.make_async_copy(x_hbm, src.at[far], local_sems.at[0]),
        pltpu.make_async_copy(wq_hbm, wq, local_sems.at[1]),
        pltpu.make_async_copy(wv_hbm, wv, local_sems.at[2]),
        pltpu.make_async_copy(mask_hbm, masks.at[0], local_sems.at[3]),
        pltpu.make_async_copy(mult_hbm, mults.at[0], local_sems.at[4]),
    ]
    local[0].start()
    barrier = pltpu.get_barrier_semaphore()
    for h in range(fars):
        @pl.when((h > far) | (h == far - 1))
        def _():
            pl.semaphore_signal(barrier, inc=1, device_id=far_id(h), device_id_type=MESH)
    for offset in near[1:]:
        pl.semaphore_signal(barrier, inc=1, device_id=near_id(*offset), device_id_type=MESH)
    for copy in local[1:]:
        copy.start()
    local[0].wait()
    pl.semaphore_wait(barrier, far + (far < top).astype(jnp.int32) + near_count - 1)

    own_ref = src.at[far]

    def down(h):
        return pltpu.make_async_remote_copy(
            src_ref=own_ref, dst_ref=own_ref, send_sem=src_send.at[0, h], recv_sem=src_recv.at[far],
            device_id=far_id(h), device_id_type=MESH)

    def up(h):
        return pltpu.make_async_remote_copy(
            src_ref=src.at[h], dst_ref=src.at[h], send_sem=src_send.at[1, h], recv_sem=src_recv.at[h],
            device_id=far_id(far + 1), device_id_type=MESH)

    def arrived(dst, sem):
        pltpu.make_async_copy(dst, dst, sem).wait()

    for h in range(fars - 1):
        pl.when(h < far)(down(h).start)
    pl.when(far < top)(lambda: up(far).start())

    copies = []
    for k, offset in reversed(list(enumerate(near))):
        if k:
            slot = near_slot(*offset)
            copies.append(pltpu.make_async_remote_copy(
                src_ref=own_ref, dst_ref=tgt.at[slot],
                send_sem=tgt_send.at[k], recv_sem=tgt_recv.at[slot],
                device_id=near_id(*offset), device_id_type=MESH))
    for k, (dm, dc) in enumerate(tables):
        if k:
            slot = tables.index((-dm % mids, -dc % cores))
            for n, (table, slots) in enumerate(((mask_hbm, masks), (mult_hbm, mults))):
                copies.append(pltpu.make_async_remote_copy(
                    src_ref=table, dst_ref=slots.at[slot],
                    send_sem=tab_send.at[n, k], recv_sem=tab_recv.at[n, slot],
                    device_id=near_id(dm, dc, 0), device_id_type=MESH))
    for copy in copies:
        copy.start()

    for h in reversed(range(fars - 1)):
        @pl.when((h < far) & (far < top))
        def _():
            arrived(src.at[h], src_recv.at[h])
            up(h).start()

    for copy in local[1:]:
        copy.wait()
    root_scale = 1.0 / x_hbm.shape[1] ** 0.5
    width = fars * TILE
    tile_count = masks.shape[2]

    def query_of(rows):
        return jnp.dot(rows, wq[...], preferred_element_type=jnp.float32).astype(jnp.bfloat16)

    def weigh(query, source, factor):
        score = lax.dot_general(query, source, (((1,), (1,)), ((), ())),
                                preferred_element_type=jnp.float32)
        score = score * factor
        return jnp.maximum(score, 0.2 * score).astype(jnp.bfloat16)

    place = lax.broadcasted_iota(jnp.int32, (tile_count, width), 1) // TILE
    tile = ((place * mids + mid) * cores + core) * rep_count + r
    one_hot = lax.broadcasted_iota(jnp.int32, (tile_count, width), 0) == tile
    one_hot = one_hot.astype(jnp.float32).astype(jnp.bfloat16)
    for k, (dm, dc) in enumerate(tables):
        if k:
            arrived(masks.at[k], tab_recv.at[0, k])
            arrived(mults.at[k], tab_recv.at[1, k])
        fac = (masks[k] * mults[k]).astype(jnp.float32).astype(jnp.bfloat16)
        wide = jnp.dot(fac, one_hot, preferred_element_type=jnp.float32) * root_scale
        rows = lax.broadcasted_iota(jnp.int32, wide.shape, 0)
        for dr in range(rep_count):
            row = jnp.sum(jnp.where(rows == (r + dr) % rep_count, wide, 0.0), axis=0, keepdims=True)
            for h in range(fars):
                factors[near.index((dm, dc, dr)), h] = row[:, h * TILE:(h + 1) * TILE]

    own = src[far]
    for k in range(near_count):
        if k:
            arrived(tgt.at[k], tgt_recv.at[k])
            rows = tgt[k]
        else:
            rows = own
        query = query_of(rows)
        queries[k] = query
        sums[k] = jnp.dot(weigh(query, own, factors[k, far]), own,
                          preferred_element_type=jnp.float32)

    at_top = (far == top).astype(jnp.int32)
    last = (1 - at_top) * top

    def await_source(h):
        @pl.when((h > far) | (far == top))
        def _():
            arrived(src.at[h], src_recv.at[h])

    rest = []
    for i in range(fars - 2):
        past = (i >= far).astype(jnp.int32)
        rest.append(i + at_top + (1 - at_top) * past)
    if rest:
        for h in rest:
            await_source(h)
        others = jnp.concatenate([src[h] for h in rest], axis=0)
        for k in range(near_count):
            factor = jnp.concatenate([factors[k, h] for h in rest], axis=1)
            sums[k] += jnp.dot(weigh(queries[k], others, factor), others,
                               preferred_element_type=jnp.float32)
    if fars > 1:
        await_source(last)
    final = src[last]
    order = sorted(range(near_count), key=lambda k: (k == 0, -sum(v > 0 for v in near[k])))
    for k in order:
        part = sums[k]
        if fars > 1:
            w = weigh(queries[k], final, factors[k, last])
            part = part + jnp.dot(w, final, preferred_element_type=jnp.float32)
        if k:
            sent[k] = part.astype(jnp.bfloat16)
            slot = near_slot(*near[k])
            copy = pltpu.make_async_remote_copy(
                src_ref=sent.at[k], dst_ref=got.at[slot],
                send_sem=sum_send.at[k], recv_sem=sum_recv.at[slot],
                device_id=near_id(*near[k]), device_id_type=MESH)
            copy.start()
            copies.append(copy)
        else:
            total = part
    for k in range(1, near_count):
        arrived(got.at[k], sum_recv.at[k])
        total = total + got[k].astype(jnp.float32)
    verts = TILE * blk_count * rep_count
    aggregate = (total * (2.0 * verts) ** (-0.5)).astype(jnp.bfloat16)
    mixed = jnp.dot(aggregate, wv[...], preferred_element_type=jnp.float32)
    out_ref[...] = (own.astype(jnp.float32) + mixed).astype(jnp.bfloat16)
    for copy in copies:
        copy.wait_send()
    for h in range(fars - 1):
        pl.when(h < far)(down(h).wait_send)
        pl.when((h <= far) & (far < top))(up(h).wait_send)


def body(blk_count, rep_count, features, tile_mask, multiplicity, w_query, w_value):
    rows, width = features.shape
    assert rows == TILE
    fars, mids, cores = split_of(blk_count)
    near_count = mids * cores * rep_count
    table_rows, table_cols = tile_mask.shape
    dma = pltpu.SemaphoreType.DMA
    return pl.pallas_call(
        functools.partial(kernel, blk_count, rep_count),
        out_shape=pltpu.VMEM((rows, width), jnp.bfloat16),
        in_specs=[pl.BlockSpec(memory_space=pl.ANY)] * 5,
        out_specs=pl.BlockSpec(memory_space=pltpu.VMEM),
        scratch_shapes=[
            pltpu.VMEM((near_count, rows, width), jnp.bfloat16),
            pltpu.VMEM((fars, rows, width), jnp.bfloat16),
            pltpu.VMEM((mids * cores, table_rows, table_cols), jnp.int32),
            pltpu.VMEM((mids * cores, table_rows, table_cols), jnp.int32),
            pltpu.VMEM(w_query.shape, jnp.bfloat16),
            pltpu.VMEM(w_value.shape, jnp.bfloat16),
            pltpu.VMEM((near_count, fars, 1, TILE), jnp.float32),
            pltpu.VMEM((near_count, rows, width), jnp.bfloat16),
            pltpu.VMEM((near_count, rows, width), jnp.float32),
            pltpu.VMEM((near_count, rows, width), jnp.bfloat16),
            pltpu.VMEM((near_count, rows, width), jnp.bfloat16),
            dma((5,)),
            dma((near_count,)), dma((near_count,)),
            dma((2, fars)), dma((fars,)),
            dma((2, mids * cores)), dma((2, mids * cores)),
            dma((near_count,)), dma((near_count,)),
        ],
        compiler_params=pltpu.CompilerParams(collective_id=0, has_side_effects=True),
    )(features, tile_mask, multiplicity, w_query, w_value)


def solution(mesh):
    in_specs = (P(("blk", "rep"), None), P("blk", None), P("blk", None), P(), P())
    out_specs = P(("blk", "rep"), None)
    run = functools.partial(body, mesh.shape["blk"], mesh.shape["rep"])
    return jax.shard_map(run, mesh=mesh, in_specs=in_specs, out_specs=out_specs, check_vma=False)
```

time: 19.7 us -> 18.4 us (0.934)
  local copies, waits for them, and re-layouts: 1.38 us -> 0.62 us
  Pallas kernels: 18.1 us -> 17.6 us
    unnamed x1, local copies, waits for them, and re-layouts: 1.38 us -> 0.62 us
    pallas_call x1, Pallas kernels: 18.1 us -> 17.6 us  [body(): pl.pallas_call(functools.partial(kernel, blk_count, rep_count), out_shape...]
where the time goes in v2:
time: 18.4 us; the launch traced here: 18.3 us
  Pallas kernels  17.6 us (96%)
  local copies, waits for them, and re-layouts  0.62 us (3%)
    pallas_call x1, Pallas kernels, body(): pl.pallas_call(functools.partial(kernel, blk_count, rep_count), out_shape...  17.6 us
    unnamed x1, local copies, waits for them, and re-layouts  0.62 us

profile of v2, /device:TPU:0, one launch (start us, length us, event | category | flops | bytes accessed | tf_op | source)
XLA Modules:
  0.0 18.3 jit_solution(2459282035840585481)
XLA Ops:
  0.0 17.6 %shard_map.55 = bf16[128,128]{1,0:T(8,128)(2,1)S(1)} custom-call(bf16[128,128]{1,0:T(8,128)(2,1)} %x_hbm.1, s32[2,32]{1,0:T(2,128)} %mask_hbm.1, s32[2,32]{1,0:T(2,128)} %mult_hbm.1, bf16[128,128]{1,0:T(8,128)(2,1)} %wq_hbm.1, bf16[128,128]{1,0:T(8,128)(2,1)} %wv_hbm.1), custom_call_target="tpu_custom_call" | custom-call | tf_op jit(solution)/shard_map/pallas_call | solution.py:217
  17.6 0.6 %copy.7 = bf16[128,128]{1,0:T(8,128)(2,1)} copy(bf16[128,128]{1,0:T(8,128)(2,1)S(1)} %shard_map.55) | data formatting | bytes 65536

commit v3 on v2

--- a/solution.py
+++ b/solution.py
@@ -23,7 +23,7 @@
     x_hbm, mask_hbm, mult_hbm, wq_hbm, wv_hbm,
     out_ref,
     tgt, src, masks, mults, wq, wv, factors, queries, sums, sent, got,
-    local_sems, tgt_send, tgt_recv, src_send, src_recv, tab_send, tab_recv, sum_send, sum_recv,
+    local_sems, tgt_send, tgt_recv, src_send, src_recv, side_send, side_recv, tab_send, tab_recv, sum_send, sum_recv,
 ):
     fars, mids, cores = split_of(blk_count)
     b = lax.axis_index("blk")
@@ -31,20 +31,21 @@
     core = b % cores
     mid = (b // cores) % mids
     far = b // (cores * mids)
-    near = list(itertools.product(range(mids), range(cores), range(rep_count)))
-    tables = list(itertools.product(range(mids), range(cores)))
+    near = list(itertools.product(range(mids), range(rep_count)))
     near_count = len(near)
     top = fars - 1
 
-    def near_id(dm, dc, dr):
-        m, c, q = (mid + dm) % mids, (core + dc) % cores, (r + dr) % rep_count
-        return ((far * mids + m) * cores + c, q)
+    def near_id(dm, dr):
+        return ((far * mids + (mid + dm) % mids) * cores + core, (r + dr) % rep_count)
 
     def far_id(h):
         return ((h * mids + mid) * cores + core, r)
 
-    def near_slot(dm, dc, dr):
-        return near.index((-dm % mids, -dc % cores, -dr % rep_count))
+    def near_slot(dm, dr):
+        return near.index((-dm % mids, -dr % rep_count))
+
+    sides = cores - 1
+    side_id = ((far * mids + mid) * cores + (core + 1) % cores, r)
 
     local = [
         pltpu.make_async_copy(x_hbm, src.at[far], local_sems.at[0]),
@@ -61,10 +62,12 @@
             pl.semaphore_signal(barrier, inc=1, device_id=far_id(h), device_id_type=MESH)
     for offset in near[1:]:
         pl.semaphore_signal(barrier, inc=1, device_id=near_id(*offset), device_id_type=MESH)
+    if sides:
+        pl.semaphore_signal(barrier, inc=1, device_id=side_id, device_id_type=MESH)
     for copy in local[1:]:
         copy.start()
     local[0].wait()
-    pl.semaphore_wait(barrier, far + (far < top).astype(jnp.int32) + near_count - 1)
+    pl.semaphore_wait(barrier, far + (far < top).astype(jnp.int32) + near_count - 1 + sides)
 
     own_ref = src.at[far]
 
@@ -77,6 +80,11 @@
         return pltpu.make_async_remote_copy(
             src_ref=src.at[h], dst_ref=src.at[h], send_sem=src_send.at[1, h], recv_sem=src_recv.at[h],
             device_id=far_id(far + 1), device_id_type=MESH)
+
+    def side(h):
+        return pltpu.make_async_remote_copy(
+            src_ref=src.at[h], dst_ref=src.at[fars + h], send_sem=side_send.at[h],
+            recv_sem=side_recv.at[h], device_id=side_id, device_id_type=MESH)
 
     def arrived(dst, sem):
         pltpu.make_async_copy(dst, dst, sem).wait()
@@ -93,27 +101,35 @@
                 src_ref=own_ref, dst_ref=tgt.at[slot],
                 send_sem=tgt_send.at[k], recv_sem=tgt_recv.at[slot],
                 device_id=near_id(*offset), device_id_type=MESH))
-    for k, (dm, dc) in enumerate(tables):
-        if k:
-            slot = tables.index((-dm % mids, -dc % cores))
+    for k in range(mids):
+        if k:
+            slot = -k % mids
             for n, (table, slots) in enumerate(((mask_hbm, masks), (mult_hbm, mults))):
                 copies.append(pltpu.make_async_remote_copy(
                     src_ref=table, dst_ref=slots.at[slot],
                     send_sem=tab_send.at[n, k], recv_sem=tab_recv.at[n, slot],
-                    device_id=near_id(dm, dc, 0), device_id_type=MESH))
+                    device_id=near_id(k, 0), device_id_type=MESH))
     for copy in copies:
         copy.start()
 
-    for h in reversed(range(fars - 1)):
-        @pl.when((h < far) & (far < top))
-        def _():
-            arrived(src.at[h], src_recv.at[h])
-            up(h).start()
+    if sides:
+        side(far).start()
+    at_top = (far == top).astype(jnp.int32)
+    last = (1 - at_top) * top
+    rest = []
+    for i in range(fars - 2):
+        below = (i < far).astype(jnp.int32)
+        h = below * (far - 1 - i) + (1 - below) * (i + 1)
+        rest.append(h)
+        arrived(src.at[h], src_recv.at[h])
+        pl.when((i < far) & (far < top))(up(h).start)
+        if sides:
+            side(h).start()
 
     for copy in local[1:]:
         copy.wait()
     root_scale = 1.0 / x_hbm.shape[1] ** 0.5
-    width = fars * TILE
+    width = cores * fars * TILE
     tile_count = masks.shape[2]
 
     def query_of(rows):
@@ -126,10 +142,11 @@
         return jnp.maximum(score, 0.2 * score).astype(jnp.bfloat16)
 
     place = lax.broadcasted_iota(jnp.int32, (tile_count, width), 1) // TILE
-    tile = ((place * mids + mid) * cores + core) * rep_count + r
+    place_core = (core + place // fars) % cores
+    tile = ((place % fars * mids + mid) * cores + place_core) * rep_count + r
     one_hot = lax.broadcasted_iota(jnp.int32, (tile_count, width), 0) == tile
     one_hot = one_hot.astype(jnp.float32).astype(jnp.bfloat16)
-    for k, (dm, dc) in enumerate(tables):
+    for k in range(mids):
         if k:
             arrived(masks.at[k], tab_recv.at[0, k])
             arrived(mults.at[k], tab_recv.at[1, k])
@@ -138,10 +155,16 @@
         rows = lax.broadcasted_iota(jnp.int32, wide.shape, 0)
         for dr in range(rep_count):
             row = jnp.sum(jnp.where(rows == (r + dr) % rep_count, wide, 0.0), axis=0, keepdims=True)
-            for h in range(fars):
-                factors[near.index((dm, dc, dr)), h] = row[:, h * TILE:(h + 1) * TILE]
+            for h in range(cores * fars):
+                factors[near.index((k, dr)), h] = row[:, h * TILE:(h + 1) * TILE]
 
     own = src[far]
+    early = [far] + rest
+    if sides:
+        for h in early:
+            arrived(src.at[fars + h], side_recv.at[h])
+        early = early + [fars + h for h in early]
+    sources = jnp.concatenate([src[h] for h in early], axis=0)
     for k in range(near_count):
         if k:
             arrived(tgt.at[k], tgt_recv.at[k])
@@ -150,31 +173,19 @@
             rows = own
         query = query_of(rows)
         queries[k] = query
-        sums[k] = jnp.dot(weigh(query, own, factors[k, far]), own,
-                          preferred_element_type=jnp.float32)
-
-    at_top = (far == top).astype(jnp.int32)
-    last = (1 - at_top) * top
-
-    def await_source(h):
-        @pl.when((h > far) | (far == top))
-        def _():
-            arrived(src.at[h], src_recv.at[h])
-
-    rest = []
-    for i in range(fars - 2):
-        past = (i >= far).astype(jnp.int32)
-        rest.append(i + at_top + (1 - at_top) * past)
-    if rest:
-        for h in rest:
-            await_source(h)
-        others = jnp.concatenate([src[h] for h in rest], axis=0)
-        for k in range(near_count):
-            factor = jnp.concatenate([factors[k, h] for h in rest], axis=1)
-            sums[k] += jnp.dot(weigh(queries[k], others, factor), others,
-                               preferred_element_type=jnp.float32)
+        factor = jnp.concatenate([factors[k, h] for h in early], axis=1)
+        sums[k] = jnp.dot(weigh(query, sources, factor), sources, preferred_element_type=jnp.float32)
+
     if fars > 1:
-        await_source(last)
+        arrived(src.at[last], src_recv.at[last])
+        if sides:
+            side(last).start()
+            first = src[last]
+            for k in range(near_count):
+                sums[k] += jnp.dot(weigh(queries[k], first, factors[k, last]), first,
+                                   preferred_element_type=jnp.float32)
+            arrived(src.at[fars + last], side_recv.at[last])
+    last = last + sides * fars
     final = src[last]
     order = sorted(range(near_count), key=lambda k: (k == 0, -sum(v > 0 for v in near[k])))
     for k in order:
@@ -205,13 +216,16 @@
     for h in range(fars - 1):
         pl.when(h < far)(down(h).wait_send)
         pl.when((h <= far) & (far < top))(up(h).wait_send)
+    if sides:
+        for h in range(fars):
+            side(h).wait_send()
 
 
 def body(blk_count, rep_count, features, tile_mask, multiplicity, w_query, w_value):
     rows, width = features.shape
     assert rows == TILE
     fars, mids, cores = split_of(blk_count)
-    near_count = mids * cores * rep_count
+    near_count = mids * rep_count
     table_rows, table_cols = tile_mask.shape
     dma = pltpu.SemaphoreType.DMA
     return pl.pallas_call(
@@ -221,12 +235,12 @@
         out_specs=pl.BlockSpec(memory_space=pltpu.VMEM),
         scratch_shapes=[
             pltpu.VMEM((near_count, rows, width), jnp.bfloat16),
-            pltpu.VMEM((fars, rows, width), jnp.bfloat16),
-            pltpu.VMEM((mids * cores, table_rows, table_cols), jnp.int32),
-            pltpu.VMEM((mids * cores, table_rows, table_cols), jnp.int32),
+            pltpu.VMEM((cores * fars, rows, width), jnp.bfloat16),
+            pltpu.VMEM((mids, table_rows, table_cols), jnp.int32),
+            pltpu.VMEM((mids, table_rows, table_cols), jnp.int32),
             pltpu.VMEM(w_query.shape, jnp.bfloat16),
             pltpu.VMEM(w_value.shape, jnp.bfloat16),
-            pltpu.VMEM((near_count, fars, 1, TILE), jnp.float32),
+            pltpu.VMEM((near_count, cores * fars, 1, TILE), jnp.float32),
             pltpu.VMEM((near_count, rows, width), jnp.bfloat16),
             pltpu.VMEM((near_count, rows, width), jnp.float32),
             pltpu.VMEM((near_count, rows, width), jnp.bfloat16),
@@ -234,7 +248,8 @@
             dma((5,)),
             dma((near_count,)), dma((near_count,)),
             dma((2, fars)), dma((fars,)),
-            dma((2, mids * cores)), dma((2, mids * cores)),
+            dma((fars,)), dma((fars,)),
+            dma((2, mids)), dma((2, mids)),
             dma((near_count,)), dma((near_count,)),
         ],
         compiler_params=pltpu.CompilerParams(collective_id=0, has_side_effects=True),

time: 18.4 us -> 18.3 us (level)
  no operation moved by 1% of the time
where the time goes in v3:
time: 18.3 us; the launch traced here: 18.1 us
  Pallas kernels  17.5 us (96%)
  local copies, waits for them, and re-layouts  0.62 us (3%)
    pallas_call x1, Pallas kernels, body(): pl.pallas_call(functools.partial(kernel, blk_count, rep_count), out_shape...  17.5 us
    unnamed x1, local copies, waits for them, and re-layouts  0.62 us

profile of v3, /device:TPU:0, one launch (start us, length us, event | category | flops | bytes accessed | tf_op | source)
XLA Modules:
  0.0 18.1 jit_solution(9554684581097089582)
XLA Ops:
  0.0 17.5 %shard_map.55 = bf16[128,128]{1,0:T(8,128)(2,1)S(1)} custom-call(bf16[128,128]{1,0:T(8,128)(2,1)} %x_hbm.1, s32[2,32]{1,0:T(2,128)} %mask_hbm.1, s32[2,32]{1,0:T(2,128)} %mult_hbm.1, bf16[128,128]{1,0:T(8,128)(2,1)} %wq_hbm.1, bf16[128,128]{1,0:T(8,128)(2,1)} %wv_hbm.1), custom_call_target="tpu_custom_call" | custom-call | tf_op jit(solution)/shard_map/pallas_call | solution.py:231
  17.5 0.6 %copy.7 = bf16[128,128]{1,0:T(8,128)(2,1)} copy(bf16[128,128]{1,0:T(8,128)(2,1)S(1)} %shard_map.55) | data formatting | bytes 65536

commit v4 on v3

--- a/solution.py
+++ b/solution.py
@@ -22,7 +22,7 @@
     blk_count, rep_count,
     x_hbm, mask_hbm, mult_hbm, wq_hbm, wv_hbm,
     out_ref,
-    tgt, src, masks, mults, wq, wv, factors, queries, sums, sent, got,
+    src, masks, mults, wq, wv, factors, queries, sums, sent, got,
     local_sems, tgt_send, tgt_recv, src_send, src_recv, side_send, side_recv, tab_send, tab_recv, sum_send, sum_recv,
 ):
     fars, mids, cores = split_of(blk_count)
@@ -67,6 +67,8 @@
     for copy in local[1:]:
         copy.start()
     local[0].wait()
+    local[1].wait()
+    queries[0] = jnp.dot(src[far], wq[...], preferred_element_type=jnp.float32).astype(jnp.bfloat16)
     pl.semaphore_wait(barrier, far + (far < top).astype(jnp.int32) + near_count - 1 + sides)
 
     own_ref = src.at[far]
@@ -98,7 +100,7 @@
         if k:
             slot = near_slot(*offset)
             copies.append(pltpu.make_async_remote_copy(
-                src_ref=own_ref, dst_ref=tgt.at[slot],
+                src_ref=queries.at[0], dst_ref=queries.at[slot],
                 send_sem=tgt_send.at[k], recv_sem=tgt_recv.at[slot],
                 device_id=near_id(*offset), device_id_type=MESH))
     for k in range(mids):
@@ -126,20 +128,22 @@
         if sides:
             side(h).start()
 
-    for copy in local[1:]:
+    for copy in local[2:]:
         copy.wait()
     root_scale = 1.0 / x_hbm.shape[1] ** 0.5
     width = cores * fars * TILE
     tile_count = masks.shape[2]
 
-    def query_of(rows):
-        return jnp.dot(rows, wq[...], preferred_element_type=jnp.float32).astype(jnp.bfloat16)
-
-    def weigh(query, source, factor):
+    def times(blocks, slots):
+        source = jnp.concatenate([src[h] for h in slots], axis=0)
+        query = queries[blocks].reshape(-1, source.shape[1])
         score = lax.dot_general(query, source, (((1,), (1,)), ((), ())),
                                 preferred_element_type=jnp.float32)
-        score = score * factor
-        return jnp.maximum(score, 0.2 * score).astype(jnp.bfloat16)
+        factor = jnp.concatenate([factors[blocks, h] for h in slots], axis=2)
+        score = score.reshape(factor.shape[0], TILE, source.shape[0]) * factor
+        score = jnp.maximum(score, 0.2 * score).astype(jnp.bfloat16)
+        part = jnp.dot(score.reshape(-1, source.shape[0]), source, preferred_element_type=jnp.float32)
+        return part.reshape(factor.shape[0], TILE, source.shape[1])
 
     place = lax.broadcasted_iota(jnp.int32, (tile_count, width), 1) // TILE
     place_core = (core + place // fars) % cores
@@ -164,37 +168,27 @@
         for h in early:
             arrived(src.at[fars + h], side_recv.at[h])
         early = early + [fars + h for h in early]
-    sources = jnp.concatenate([src[h] for h in early], axis=0)
-    for k in range(near_count):
-        if k:
-            arrived(tgt.at[k], tgt_recv.at[k])
-            rows = tgt[k]
-        else:
-            rows = own
-        query = query_of(rows)
-        queries[k] = query
-        factor = jnp.concatenate([factors[k, h] for h in early], axis=1)
-        sums[k] = jnp.dot(weigh(query, sources, factor), sources, preferred_element_type=jnp.float32)
+    sums[:1] = times(slice(0, 1), early)
+    for k in range(1, near_count):
+        arrived(queries.at[k], tgt_recv.at[k])
+    if near_count > 1:
+        sums[1:] = times(slice(1, near_count), early)
 
     if fars > 1:
         arrived(src.at[last], src_recv.at[last])
         if sides:
             side(last).start()
-            first = src[last]
-            for k in range(near_count):
-                sums[k] += jnp.dot(weigh(queries[k], first, factors[k, last]), first,
-                                   preferred_element_type=jnp.float32)
+            sums[...] += times(slice(0, near_count), [last])
             arrived(src.at[fars + last], side_recv.at[last])
     last = last + sides * fars
-    final = src[last]
+    parts = sums[...]
+    if fars > 1:
+        parts = parts + times(slice(0, near_count), [last])
     order = sorted(range(near_count), key=lambda k: (k == 0, -sum(v > 0 for v in near[k])))
+    sent[...] = parts.astype(jnp.bfloat16)
+    total = parts[0]
     for k in order:
-        part = sums[k]
-        if fars > 1:
-            w = weigh(queries[k], final, factors[k, last])
-            part = part + jnp.dot(w, final, preferred_element_type=jnp.float32)
-        if k:
-            sent[k] = part.astype(jnp.bfloat16)
+        if k:
             slot = near_slot(*near[k])
             copy = pltpu.make_async_remote_copy(
                 src_ref=sent.at[k], dst_ref=got.at[slot],
@@ -202,8 +196,6 @@
                 device_id=near_id(*near[k]), device_id_type=MESH)
             copy.start()
             copies.append(copy)
-        else:
-            total = part
     for k in range(1, near_count):
         arrived(got.at[k], sum_recv.at[k])
         total = total + got[k].astype(jnp.float32)
@@ -234,7 +226,6 @@
         in_specs=[pl.BlockSpec(memory_space=pl.ANY)] * 5,
         out_specs=pl.BlockSpec(memory_space=pltpu.VMEM),
         scratch_shapes=[
-            pltpu.VMEM((near_count, rows, width), jnp.bfloat16),
             pltpu.VMEM((cores * fars, rows, width), jnp.bfloat16),
             pltpu.VMEM((mids, table_rows, table_cols), jnp.int32),
             pltpu.VMEM((mids, table_rows, table_cols), jnp.int32),

time: 18.3 us -> 17.5 us (0.956)
  Pallas kernels: 17.5 us -> 16.7 us
    pallas_call x1, Pallas kernels: 17.5 us -> 16.7 us  [body(): pl.pallas_call(functools.partial(kernel, blk_count, rep_count), out_shape...]
where the time goes in v4:
time: 17.5 us; the launch traced here: 17.3 us
  Pallas kernels  16.7 us (95%)
  local copies, waits for them, and re-layouts  0.62 us (4%)
    pallas_call x1, Pallas kernels, body(): pl.pallas_call(functools.partial(kernel, blk_count, rep_count), out_shape...  16.7 us
    unnamed x1, local copies, waits for them, and re-layouts  0.62 us

profile of v4, /device:TPU:0, one launch (start us, length us, event | category | flops | bytes accessed | tf_op | source)
XLA Modules:
  0.0 17.3 jit_solution(10929165286058782476)
XLA Ops:
  0.0 16.7 %shard_map.55 = bf16[128,128]{1,0:T(8,128)(2,1)S(1)} custom-call(bf16[128,128]{1,0:T(8,128)(2,1)} %x_hbm.1, s32[2,32]{1,0:T(2,128)} %mask_hbm.1, s32[2,32]{1,0:T(2,128)} %mult_hbm.1, bf16[128,128]{1,0:T(8,128)(2,1)} %wq_hbm.1, bf16[128,128]{1,0:T(8,128)(2,1)} %wv_hbm.1), custom_call_target="tpu_custom_call" | custom-call | tf_op jit(solution)/shard_map/pallas_call | solution.py:223
  16.7 0.6 %copy.7 = bf16[128,128]{1,0:T(8,128)(2,1)} copy(bf16[128,128]{1,0:T(8,128)(2,1)S(1)} %shard_map.55) | data formatting | bytes 65536

commit v5 on v4

--- a/solution.py
+++ b/solution.py
@@ -23,7 +23,7 @@
     x_hbm, mask_hbm, mult_hbm, wq_hbm, wv_hbm,
     out_ref,
     src, masks, mults, wq, wv, factors, queries, sums, sent, got,
-    local_sems, tgt_send, tgt_recv, src_send, src_recv, side_send, side_recv, tab_send, tab_recv, sum_send, sum_recv,
+    local_sems, tgt_send, tgt_recv, src_send, src_recv, side_send, side_recv, tab_send, tab_recv, sum_send, sum_recv, row_sem,
 ):
     fars, mids, cores = split_of(blk_count)
     b = lax.axis_index("blk")
@@ -33,6 +33,8 @@
     far = b // (cores * mids)
     near = list(itertools.product(range(mids), range(rep_count)))
     near_count = len(near)
+    direct = [(dm, dr) for dm, dr in near if (dm == 0) != (dr == 0)]
+    crossed = [(dm, dr) for dm, dr in near if dm and dr]
     top = fars - 1
 
     def near_id(dm, dr):
@@ -60,7 +62,7 @@
         @pl.when((h > far) | (h == far - 1))
         def _():
             pl.semaphore_signal(barrier, inc=1, device_id=far_id(h), device_id_type=MESH)
-    for offset in near[1:]:
+    for offset in direct:
         pl.semaphore_signal(barrier, inc=1, device_id=near_id(*offset), device_id_type=MESH)
     if sides:
         pl.semaphore_signal(barrier, inc=1, device_id=side_id, device_id_type=MESH)
@@ -69,7 +71,10 @@
     local[0].wait()
     local[1].wait()
     queries[0] = jnp.dot(src[far], wq[...], preferred_element_type=jnp.float32).astype(jnp.bfloat16)
-    pl.semaphore_wait(barrier, far + (far < top).astype(jnp.int32) + near_count - 1 + sides)
+    pl.semaphore_wait(barrier, far + (far < top).astype(jnp.int32) + len(direct) + sides)
+    if crossed:
+        for dm in range(1, mids):
+            pl.semaphore_signal(row_sem, inc=1, device_id=near_id(dm, 0), device_id_type=MESH)
 
     own_ref = src.at[far]
 
@@ -96,8 +101,10 @@
     pl.when(far < top)(lambda: up(far).start())
 
     copies = []
-    for k, offset in reversed(list(enumerate(near))):
-        if k:
+
+    def send_queries(offsets):
+        for offset in offsets:
+            k = near.index(offset)
             slot = near_slot(*offset)
             copies.append(pltpu.make_async_remote_copy(
                 src_ref=queries.at[0], dst_ref=queries.at[slot],
@@ -111,11 +118,17 @@
                     src_ref=table, dst_ref=slots.at[slot],
                     send_sem=tab_send.at[n, k], recv_sem=tab_recv.at[n, slot],
                     device_id=near_id(k, 0), device_id_type=MESH))
+    send_queries(direct)
     for copy in copies:
         copy.start()
-
     if sides:
         side(far).start()
+    if crossed:
+        pl.semaphore_wait(row_sem, mids - 1)
+        crossed_from = len(copies)
+        send_queries(crossed)
+        for copy in copies[crossed_from:]:
+            copy.start()
     at_top = (far == top).astype(jnp.int32)
     last = (1 - at_top) * top
     rest = []
@@ -242,6 +255,7 @@
             dma((fars,)), dma((fars,)),
             dma((2, mids)), dma((2, mids)),
             dma((near_count,)), dma((near_count,)),
+            pltpu.SemaphoreType.REGULAR,
         ],
         compiler_params=pltpu.CompilerParams(collective_id=0, has_side_effects=True),
     )(features, tile_mask, multiplicity, w_query, w_value)

time: 17.5 us -> 17.5 us (level)
  no operation moved by 1% of the time
where the time goes in v5:
time: 17.5 us; the launch traced here: 17.3 us
  Pallas kernels  16.7 us (95%)
  local copies, waits for them, and re-layouts  0.62 us (4%)
    pallas_call x1, Pallas kernels, body(): pl.pallas_call(functools.partial(kernel, blk_count, rep_count), out_shape...  16.7 us
    unnamed x1, local copies, waits for them, and re-layouts  0.62 us

profile of v5, /device:TPU:0, one launch (start us, length us, event | category | flops | bytes accessed | tf_op | source)
XLA Modules:
  0.0 17.3 jit_solution(1324193462454570530)
XLA Ops:
  0.0 16.7 %shard_map.55 = bf16[128,128]{1,0:T(8,128)(2,1)S(1)} custom-call(bf16[128,128]{1,0:T(8,128)(2,1)} %x_hbm.1, s32[2,32]{1,0:T(2,128)} %mask_hbm.1, s32[2,32]{1,0:T(2,128)} %mult_hbm.1, bf16[128,128]{1,0:T(8,128)(2,1)} %wq_hbm.1, bf16[128,128]{1,0:T(8,128)(2,1)} %wv_hbm.1), custom_call_target="tpu_custom_call" | custom-call | tf_op jit(solution)/shard_map/pallas_call | solution.py:236
  16.7 0.6 %copy.7 = bf16[128,128]{1,0:T(8,128)(2,1)} copy(bf16[128,128]{1,0:T(8,128)(2,1)S(1)} %shard_map.55) | data formatting | bytes 65536

commit v6 on v5

--- a/solution.py
+++ b/solution.py
@@ -93,11 +93,21 @@
             src_ref=src.at[h], dst_ref=src.at[fars + h], send_sem=side_send.at[h],
             recv_sem=side_recv.at[h], device_id=side_id, device_id_type=MESH)
 
+    hop = fars > 2
+
+    def goes_down(h):
+        return (h < far) & ((far < top) | (h != top - 2)) if hop else h < far
+
+    def pass_down():
+        return pltpu.make_async_remote_copy(
+            src_ref=src.at[top], dst_ref=src.at[top], send_sem=src_send.at[0, top],
+            recv_sem=src_recv.at[top], device_id=far_id(top - 2), device_id_type=MESH)
+
     def arrived(dst, sem):
         pltpu.make_async_copy(dst, dst, sem).wait()
 
     for h in range(fars - 1):
-        pl.when(h < far)(down(h).start)
+        pl.when(goes_down(h))(down(h).start)
     pl.when(far < top)(lambda: up(far).start())
 
     copies = []
@@ -141,6 +151,12 @@
         if sides:
             side(h).start()
 
+    if hop:
+        @pl.when(far == top - 1)
+        def _():
+            arrived(src.at[top], src_recv.at[top])
+            pass_down().start()
+
     for copy in local[2:]:
         copy.wait()
     root_scale = 1.0 / x_hbm.shape[1] ** 0.5
@@ -188,7 +204,12 @@
         sums[1:] = times(slice(1, near_count), early)
 
     if fars > 1:
-        arrived(src.at[last], src_recv.at[last])
+        if hop:
+            @pl.when(far != top - 1)
+            def _():
+                arrived(src.at[last], src_recv.at[last])
+        else:
+            arrived(src.at[last], src_recv.at[last])
         if sides:
             side(last).start()
             sums[...] += times(slice(0, near_count), [last])
@@ -219,8 +240,10 @@
     for copy in copies:
         copy.wait_send()
     for h in range(fars - 1):
-        pl.when(h < far)(down(h).wait_send)
+        pl.when(goes_down(h))(down(h).wait_send)
         pl.when((h <= far) & (far < top))(up(h).wait_send)
+    if hop:
+        pl.when(far == top - 1)(pass_down().wait_send)
     if sides:
         for h in range(fars):
             side(h).wait_send()

time: 17.5 us -> 16.7 us (0.954)
  the two profiles are of different devices: /device:TPU:0 before, /device:TPU:9 now
where the time goes in v6:
time: 16.7 us; the launch traced here: 16.5 us
  Pallas kernels  15.9 us (95%)
  local copies, waits for them, and re-layouts  0.62 us (4%)
    pallas_call x1, Pallas kernels, body(): pl.pallas_call(functools.partial(kernel, blk_count, rep_count), out_shape...  15.9 us
    unnamed x1, local copies, waits for them, and re-layouts  0.62 us

profile of v6, /device:TPU:9, one launch (start us, length us, event | category | flops | bytes accessed | tf_op | source)
XLA Modules:
  0.0 16.5 jit_solution(14494986551624414085)
XLA Ops:
  0.0 15.9 %shard_map.55 = bf16[128,128]{1,0:T(8,128)(2,1)S(1)} custom-call(bf16[128,128]{1,0:T(8,128)(2,1)} %x_hbm.1, s32[2,32]{1,0:T(2,128)} %mask_hbm.1, s32[2,32]{1,0:T(2,128)} %mult_hbm.1, bf16[128,128]{1,0:T(8,128)(2,1)} %wq_hbm.1, bf16[128,128]{1,0:T(8,128)(2,1)} %wv_hbm.1), custom_call_target="tpu_custom_call" | custom-call | tf_op jit(solution)/shard_map/pallas_call | solution.py:259
  15.9 0.6 %copy.7 = bf16[128,128]{1,0:T(8,128)(2,1)} copy(bf16[128,128]{1,0:T(8,128)(2,1)S(1)} %shard_map.55) | data formatting | bytes 65536
